TPU v7x, 32 devices: a whole 2x2x4 slice. The times are simulated.
32 devices in a mesh: groups: 2 (over x), ctx: 16 (over z, y, core).
Axes of the slice: x: 2, y: 2, z: 4, core: 2. Of those that a mesh axis runs over, the one named last changes fastest.
Arguments:
- queries: bfloat16 [4096, 8192], P(('groups', 'ctx')), parts along dimension 0, may hold values from -8 to 8
- new_keys: bfloat16 [4096, 1024], P(('groups', 'ctx')), parts along dimension 0, may hold values from -12 to 12
- new_values: bfloat16 [4096, 1024], P(('groups', 'ctx')), parts along dimension 0, may hold values from -6 to 6
- prefix_keys: bfloat16 [256, 1024], P(('groups', 'ctx')), parts along dimension 0, may hold values from -16 to 16
- prefix_values: bfloat16 [256, 1024], P(('groups', 'ctx')), parts along dimension 0, may hold values from -6 to 6
- pool_keys: bfloat16 [32, 2, 256, 1024], P(('groups', 'ctx')), parts along dimension 0, may hold values from -12 to 12
- pool_values: bfloat16 [32, 2, 256, 1024], P(('groups', 'ctx')), parts along dimension 0, may hold values from -6 to 6
- owners: int32 [4], P('groups'), parts along dimension 0, may hold values from 0 to 15
- lengths: int32 [32], P(('groups', 'ctx')), parts along dimension 0, may hold values from 1 to 128, as said below
Outputs:
- attended: bfloat16 [4096, 8192], P(('groups', 'ctx')), parts along dimension 0
There are 2 independent parts, one for each index of `groups`. A program takes and returns all parts, laid end to end along the dimension named above; each array names one. Nothing has to cross between parts.
Inputs may be any that keep to these rules, and one draw needn't show every extreme that they name: `lengths`: some device's prompt fills all 128 slots.
All inputs are finite; a program needn't handle non-finite values.
Results may differ from a plain program's by a relative error of at most 0.0035.
Values may be sent and summed in bfloat16 or wider, within the bound.
A program may use at most 128 MiB of HBM per device.

v0:
```python
import jax
import jax.numpy as jnp
from jax import lax
from jax.sharding import PartitionSpec as P

H = 64
KVH = 8
HD = 128
SB = 2
BLK = 256


def attend(carried, head_queries, key_rows, value_rows, visible):
    maxima, totals, accums = carried
    new_maxima = []
    new_totals = []
    new_accums = []
    score_scale = 1.0 / HD**0.5
    for kv_head in range(KVH):
        head_keys = key_rows[:, kv_head * HD : (kv_head + 1) * HD]
        head_values = value_rows[:, kv_head * HD : (kv_head + 1) * HD]
        scores = (
            lax.dot_general(
                head_queries[kv_head],
                head_keys,
                (((1,), (1,)), ((), ())),
                preferred_element_type=jnp.float32,
            )
            * score_scale
        )
        if visible is not None:
            scores = jnp.where(visible, scores, -1e30)
        new_max = jnp.maximum(maxima[kv_head], jnp.max(scores, axis=1))
        weights = jnp.exp(scores - new_max[:, None])
        if visible is not None:
            weights = jnp.where(visible, weights, 0.0)
        shrink = jnp.exp(maxima[kv_head] - new_max)
        new_totals.append(totals[kv_head] * shrink + jnp.sum(weights, axis=1))
        summed = jnp.dot(
            weights.astype(jnp.bfloat16), head_values, preferred_element_type=jnp.float32
        )
        new_accums.append(accums[kv_head] * shrink[:, None] + summed)
        new_maxima.append(new_max)
    return (jnp.stack(new_maxima), jnp.stack(new_totals), jnp.stack(new_accums))


def body(
    queries,
    new_keys,
    new_values,
    prefix_keys,
    prefix_values,
    pool_keys,
    pool_values,
    owners,
    lengths,
):
    group_size = H // KVH
    rows_here = queries.shape[0]
    head_queries = [
        queries[:, kv_head * group_size * HD : (kv_head + 1) * group_size * HD].reshape(
            rows_here * group_size, HD
        )
        for kv_head in range(KVH)
    ]
    carried = (
        jnp.full((KVH, rows_here * group_size), -1e30, jnp.float32),
        jnp.zeros((KVH, rows_here * group_size), jnp.float32),
        jnp.zeros((KVH, rows_here * group_size, HD), jnp.float32),
    )
    length = lengths[0]
    positions = jnp.arange(rows_here)
    own_visible = (positions[None, :] <= positions[:, None]) & (positions[None, :] < length)
    own_visible = jnp.repeat(own_visible, group_size, axis=0)
    carried = attend(carried, head_queries, new_keys, new_values, own_visible)
    pages_keys = pool_keys[0]
    pages_values = pool_values[0]
    my_rank = lax.axis_index("ctx")
    owned = (owners == my_rank)[:, None, None]
    mine_keys = jnp.where(owned, pages_keys.astype(jnp.float32), 0.0).reshape(SB * BLK, KVH * HD)
    mine_values = jnp.where(owned, pages_values.astype(jnp.float32), 0.0).reshape(
        SB * BLK, KVH * HD
    )
    part_keys, part_values = (
        lax.psum_scatter(mine_keys, "ctx", scatter_dimension=0, tiled=True),
        lax.psum_scatter(mine_values, "ctx", scatter_dimension=0, tiled=True),
    )
    shared_keys, shared_values = (
        lax.all_gather(part_keys.astype(jnp.bfloat16), "ctx", axis=0, tiled=True),
        lax.all_gather(part_values.astype(jnp.bfloat16), "ctx", axis=0, tiled=True),
    )
    carried = attend(carried, head_queries, shared_keys, shared_values, None)
    whole_keys, whole_values = (
        lax.all_gather(prefix_keys, "ctx", axis=0, tiled=True),
        lax.all_gather(prefix_values, "ctx", axis=0, tiled=True),
    )
    carried = attend(carried, head_queries, whole_keys, whole_values, None)
    maxima, totals, accums = carried
    pieces = [
        (accums[kv_head] / totals[kv_head][:, None]).reshape(rows_here, group_size * HD)
        for kv_head in range(KVH)
    ]
    joined = jnp.concatenate(pieces, axis=1)
    live = positions < length
    return jnp.where(live[:, None], joined, 0.0).astype(jnp.bfloat16)


def solution(mesh):
    placed = (
        P(("groups", "ctx"), None),
        P(("groups", "ctx"), None),
        P(("groups", "ctx"), None),
        P(("groups", "ctx"), None),
        P(("groups", "ctx"), None),
        P(("groups", "ctx"), None, None, None),
        P(("groups", "ctx"), None, None, None),
        P("groups"),
        P(("groups", "ctx")),
    )
    return jax.shard_map(
        body, mesh=mesh, in_specs=placed, out_specs=P(("groups", "ctx"), None), check_vma=False
    )
```

profile of v0, /device:TPU:0, one launch (start us, length us, event | category | flops | bytes accessed | tf_op | source)
XLA Modules:
  0.0 285.9 jit_solution(6476662964461193253)
XLA Ops:
  7.3 3.9 %convert_select_fusion = (f32[512,1024]{1,0:T(8,128)}, f32[512,1024]{1,0:T(8,128)}) fusion(bf16[1,2,256,1024]{3,2,1,0:T(8,128)(2,1)} %param.15, pred[512]{0:T(512)(128)(4,1)S(1)} %broadcast_in_dim.53, bf16[1,2,256,1024]{3,2,1,0:T(8,128)(2,1)} %param.14), kind=kLoop, calls=%fused_computation.1 | loop fusion | flops 2097152 | bytes 6291968 | tf_op jit(solution)/shard_map/jit(_where)/select_n | solution.py:81
  15.4 23.8 %all_gather.14 = bf16[128,1024]{1,0:T(8,128)(2,1)S(1)} all-gather(bf16[8,1024]{1,0:T(8,128)(2,1)S(1)} %copy-done.97), channel_id=1, replica_groups=mesh['groups'=2,'ctx'=16] {'ctx'}, dimensions={0}, use_global_device_ids=true | all-gather | bytes 278528 | tf_op jit(solution)/shard_map/all_gather | solution.py:94
  48.9 27.0 %reduce-scatter.3.cloned.1.call-done = f32[32,1024]{1,0:T(8,128)} async-done(((f32[512,1024]{1,0:T(8,128)}), f32[32,1024]{1,0:T(8,128)}) %reduce-scatter.3.cloned.1.call-update) | async-done | bytes 131088 | tf_op jit(solution)/shard_map/reduce_scatter | solution.py:85
  77.5 21.8 %all_gather.15 = bf16[128,1024]{1,0:T(8,128)(2,1)} all-gather(bf16[8,1024]{1,0:T(8,128)(2,1)} %param.13), channel_id=1, replica_groups=mesh['groups'=2,'ctx'=16] {'ctx'}, dimensions={0}, use_global_device_ids=true | all-gather | bytes 278528 | tf_op jit(solution)/shard_map/all_gather | solution.py:95
  112.9 27.5 %reduce-scatter.5.cloned.1.call-done = f32[32,1024]{1,0:T(8,128)} async-done(((f32[512,1024]{1,0:T(8,128)}), f32[32,1024]{1,0:T(8,128)}) %reduce-scatter.5.cloned.1.call-update) | async-done | bytes 131088 | tf_op jit(solution)/shard_map/reduce_scatter | solution.py:86
  142.0 37.4 %all-gather.3.cloned.1.call-done = bf16[512,1024]{1,0:T(8,128)(2,1)} async-done(((bf16[32,1024]{1,0:T(8,128)(2,1)}), bf16[512,1024]{1,0:T(8,128)(2,1)}) %all-gather.3.cloned.1.call-update) | async-done | bytes 1048592 | tf_op jit(solution)/shard_map/all_gather | solution.py:89
  184.0 2.1 fusion.120
  186.2 2.8 multiply_reduce_fusion.1
  197.5 1.8 multiply_reduce_fusion.4
  200.6 1.8 multiply_reduce_fusion.5
  215.6 2.0 fusion.41
  218.2 3.3 %fusion.54 = bf16[1024,128]{1,0:T(8,128)(2,1)} fusion(f32[1024,128]{1,0:T(8,128)} %fusion.132, f32[1024,128]{1,0:T(8,128)} %fusion.41, f32[512,1024]{1,0:T(8,128)} %copy-done.6, f32[1024]{0:T(1024)S(1)} %copy-done.84, f32[1024]{0:T(1024)S(1)} %get-tuple-element.43, f32[1024]{0:T(1024)S(1)} %get-tuple-element.44, ...), kind=kOutput, calls=%fused_computation.105 | convolution fusion | flops 136445952 | bytes 3551232 | tf_op jit(solution)/shard_map/dot_general | solution.py:39
  222.6 2.1 fusion.4
  227.0 2.5 fusion.53
  231.3 2.1 fusion.6
  235.6 2.3 fusion.52
  239.7 2.1 fusion.8
  244.1 2.3 fusion.51
  248.2 2.1 fusion.10
  252.6 2.3 fusion.50
  256.7 2.1 fusion.12
  261.1 2.3 fusion.49
  270.0 2.0 fusion
  273.4 2.3 fusion.55
  (306 shorter events, 89.2 us)
Async XLA Ops:
  6.5 69.4 %reduce-scatter.3.cloned.1.call-start = ((), (), s32[]{:S(2)}) async-start(), calls=%async_computation.2 | async-start | bytes 2228224 | tf_op jit(solution)/shard_map/reduce_scatter | solution.py:85
  11.2 129.2 %reduce-scatter.5.cloned.1.call-start = ((), (), s32[]{:S(2)}) async-start(), calls=%async_computation.4 | async-start | bytes 2228224 | tf_op jit(solution)/shard_map/reduce_scatter | solution.py:86
  12.0 167.4 %all-gather.3.cloned.1.call-start = ((), (), s32[]{:S(2)}) async-start(), calls=%async_computation.3 | async-start | bytes 1114112 | tf_op jit(solution)/shard_map/all_gather | solution.py:89
  14.7 27.2 %copy-start.52 = (bf16[128,1024]{1,0:T(8,128)(2,1)S(1)}, bf16[128,1024]{1,0:T(8,128)(2,1)}, u32[]{:S(2)}) copy-start(bf16[128,1024]{1,0:T(8,128)(2,1)} %param.10) | copy-start | bytes 786436
  14.8 32.4 %copy-start.20 = (bf16[1024,128]{1,0:T(8,128)(2,1)}, bf16[1024,128]{1,0:T(8,128)(2,1)S(1)}, u32[]{:S(2)}) copy-start(bf16[1024,128]{1,0:T(8,128)(2,1)S(1)} %reshape.484) | copy-start | bytes 786436
  15.1 28.1 %copy-start.27 = (bf16[1024,128]{1,0:T(8,128)(2,1)}, bf16[1024,128]{1,0:T(8,128)(2,1)S(1)}, u32[]{:S(2)}) copy-start(bf16[1024,128]{1,0:T(8,128)(2,1)S(1)} %reshape.494) | copy-start | bytes 786436
  15.4 29.4 %copy-start.24 = (bf16[1024,128]{1,0:T(8,128)(2,1)}, bf16[1024,128]{1,0:T(8,128)(2,1)S(1)}, u32[]{:S(2)}) copy-start(bf16[1024,128]{1,0:T(8,128)(2,1)S(1)} %reshape.492) | copy-start | bytes 786436
  42.9 146.0 %copy-start.70 = (f32[1024]{0:T(1024)}, f32[1024]{0:T(1024)S(1)}, u32[]{:S(2)}) copy-start(f32[1024]{0:T(1024)S(1)} %get-tuple-element.95) | copy-start | bytes 12292
  43.2 137.8 %copy-start.68 = (f32[1024]{0:T(1024)}, f32[1024]{0:T(1024)S(1)}, u32[]{:S(2)}) copy-start(f32[1024]{0:T(1024)S(1)} %get-tuple-element.89) | copy-start | bytes 12292
  43.2 56.2 %copy-start.38 = (bf16[128,1024]{1,0:T(8,128)(2,1)S(1)}, bf16[128,1024]{1,0:T(8,128)(2,1)}, u32[]{:S(2)}) copy-start(bf16[128,1024]{1,0:T(8,128)(2,1)} %get-tuple-element.53) | copy-start | bytes 786436
  44.8 54.7 %copy-start.37 = (bf16[128,1024]{1,0:T(8,128)(2,1)S(1)}, bf16[128,1024]{1,0:T(8,128)(2,1)}, u32[]{:S(2)}) copy-start(bf16[128,1024]{1,0:T(8,128)(2,1)} %get-tuple-element.54) | copy-start | bytes 786436
  44.8 54.8 %copy-start.36 = (bf16[128,1024]{1,0:T(8,128)(2,1)S(1)}, bf16[128,1024]{1,0:T(8,128)(2,1)}, u32[]{:S(2)}) copy-start(bf16[128,1024]{1,0:T(8,128)(2,1)} %get-tuple-element.55) | copy-start | bytes 786436
  45.7 54.1 %copy-start.35 = (bf16[128,1024]{1,0:T(8,128)(2,1)S(1)}, bf16[128,1024]{1,0:T(8,128)(2,1)}, u32[]{:S(2)}) copy-start(bf16[128,1024]{1,0:T(8,128)(2,1)} %get-tuple-element.56) | copy-start | bytes 786436
  77.5 140.7 %all-gather.5.cloned.1.call-start = ((), (), s32[]{:S(2)}) async-start(), calls=%async_computation.5 | async-start | bytes 1114112 | tf_op jit(solution)/shard_map/all_gather | solution.py:90
  99.5 11.8 %copy-start.22 = (bf16[1024,128]{1,0:T(8,128)(2,1)}, bf16[1024,128]{1,0:T(8,128)(2,1)S(1)}, u32[]{:S(2)}) copy-start(bf16[1024,128]{1,0:T(8,128)(2,1)S(1)} %reshape.482) | copy-start | bytes 786436
  99.6 8.4 %copy-start.30 = (bf16[1024,128]{1,0:T(8,128)(2,1)}, bf16[1024,128]{1,0:T(8,128)(2,1)S(1)}, u32[]{:S(2)}) copy-start(bf16[1024,128]{1,0:T(8,128)(2,1)S(1)} %reshape.490) | copy-start | bytes 786436
  180.9 8.6 %copy-start.19 = (f32[1024,128]{0,1:T(8,128)S(1)}, f32[1024,128]{0,1:T(8,128)}, u32[]{:S(2)}) copy-start(f32[1024,128]{0,1:T(8,128)} %get-tuple-element.92) | copy-start | bytes 1572868
  182.3 24.9 %copy-start.56 = (f32[1024]{0:T(1024)}, f32[1024]{0:T(1024)S(1)}, u32[]{:S(2)}) copy-start(f32[1024]{0:T(1024)S(1)} %get-tuple-element.62) | copy-start | bytes 12292
  189.6 17.6 %copy-start.58 = (f32[1024]{0:T(1024)}, f32[1024]{0:T(1024)S(1)}, u32[]{:S(2)}) copy-start(f32[1024]{0:T(1024)S(1)} %get-tuple-element.64) | copy-start | bytes 12292
  193.7 13.5 %copy-start.62 = (f32[1024]{0:T(1024)}, f32[1024]{0:T(1024)S(1)}, u32[]{:S(2)}) copy-start(f32[1024]{0:T(1024)S(1)} %get-tuple-element.66) | copy-start | bytes 12292
  196.8 10.4 %copy-start.63 = (f32[1024]{0:T(1024)}, f32[1024]{0:T(1024)S(1)}, u32[]{:S(2)}) copy-start(f32[1024]{0:T(1024)S(1)} %get-tuple-element.68) | copy-start | bytes 12292
  196.8 13.5 %copy-start.53 = (f32[1024]{0:T(1024)}, f32[1024]{0:T(1024)S(1)}, u32[]{:S(2)}) copy-start(f32[1024]{0:T(1024)S(1)} %get-tuple-element.31) | copy-start | bytes 12292
  199.9 11.4 %copy-start.54 = (f32[1024]{0:T(1024)}, f32[1024]{0:T(1024)S(1)}, u32[]{:S(2)}) copy-start(f32[1024]{0:T(1024)S(1)} %get-tuple-element.36) | copy-start | bytes 12292
  203.0 9.4 %copy-start.55 = (f32[1024]{0:T(1024)}, f32[1024]{0:T(1024)S(1)}, u32[]{:S(2)}) copy-start(f32[1024]{0:T(1024)S(1)} %get-tuple-element.41) | copy-start | bytes 12292
  (80 other events, 273.9 us)
Sparse Core Ops, SparseCore 0:
  11.4 64.5 reduce-scatter.2
  79.7 60.6 reduce-scatter.4
  142.6 36.7 all-gather.2
  181.4 36.7 all-gather.4
where the time goes:
time: 287 us; the launch traced here: 286 us
  waiting for transfers between devices  93.3 us (33%)
  matrix products  76.8 us (27%)
  blocking collectives  45.6 us (16%)
  other arithmetic  38.8 us (14%)
  local copies, waits for them, and re-layouts  16.5 us (6%)
  between operations  14.9 us (5%)
    dot_general x24, matrix products, attend(): jnp.dot(weights.astype(jnp.bfloat16), head_values, preferred_element_type...  40.5 us
    all_gather x1, waiting for transfers between devices, body(): lax.all_gather(part_keys.astype(jnp.bfloat16), 'ctx', axis=0, tiled=True)  37.4 us
    dot_general x24, matrix products, attend(): lax.dot_general(head_queries[kv_head], head_keys, (((1,), (1,)), ((), ())...  36.3 us
    reduce_scatter x1, waiting for transfers between devices, body(): lax.psum_scatter(mine_values, 'ctx', scatter_dimension=0, tiled=True)  27.5 us
    reduce_scatter x1, waiting for transfers between devices, body(): lax.psum_scatter(mine_keys, 'ctx', scatter_dimension=0, tiled=True)  27 us
    all_gather x1, blocking collectives, body(): lax.all_gather(prefix_keys, 'ctx', axis=0, tiled=True)  23.8 us
    all_gather x1, blocking collectives, body(): lax.all_gather(prefix_values, 'ctx', axis=0, tiled=True)  21.8 us
    reduce_sum x16, other arithmetic, attend(): new_totals.append(totals[kv_head] * shrink + jnp.sum(weights, axis=1))  20.7 us
  transfers between devices with their start and end apart: 4, of which 4 were waited for; matrix products, arithmetic and copies ran while one was open for 23% of the time, Pallas kernels for 0%

commit v1 on v0

--- a/solution.py
+++ b/solution.py
@@ -92,7 +92,9 @@
     carried = attend(carried, head_queries, shared_keys, shared_values, None)
     whole_keys, whole_values = (
         lax.all_gather(prefix_keys, "ctx", axis=0, tiled=True),
-        lax.all_gather(prefix_values, "ctx", axis=0, tiled=True),
+        jnp.concatenate(
+            lax.all_to_all(jnp.stack([prefix_values] * lax.axis_size("ctx")), "ctx", 0, 0), axis=0
+        ),
     )
     carried = attend(carried, head_queries, whole_keys, whole_values, None)
     maxima, totals, accums = carried

time: 287 us -> 294 us (1.024)
  blocking collectives: 45.6 us -> 22.5 us
  waiting for transfers between devices: 93.3 us -> 107 us
  starting transfers between devices: 0.12 us -> 7.77 us
  matrix products: 76.8 us -> 82.2 us
    all_gather x1 -> x0, blocking collectives: 21.8 us -> none  [body(): lax.all_gather(prefix_values, 'ctx', axis=0, tiled=True)]
    reduce_scatter x1, waiting for transfers between devices: 27.5 us -> 47.5 us  [body(): lax.psum_scatter(mine_values, 'ctx', scatter_dimension=0, tiled=True)]
    all_to_all x0 -> x1, starting transfers between devices: none -> 7.46 us  [body(): lax.all_to_all(jnp.stack([prefix_values] * lax.axis_size('ctx')), 'ctx',...]
    dot_general x24, matrix products: 40.5 us -> 45.9 us  [attend(): jnp.dot(weights.astype(jnp.bfloat16), head_values, preferred_element_type...]
    reduce_scatter x1, waiting for transfers between devices: 27 us -> 21.8 us  [body(): lax.psum_scatter(mine_keys, 'ctx', scatter_dimension=0, tiled=True)]
  transfers between devices with their start and end apart: 4 -> 5, of which waited for: 4 -> 3; matrix products, arithmetic and copies ran while one was open for 23% -> 24% of each run, Pallas kernels for 0% -> 0%
where the time goes in v1:
time: 294 us; the launch traced here: 292 us
  waiting for transfers between devices  107 us (36%)
  matrix products  82.2 us (28%)
  other arithmetic  38.8 us (13%)
  blocking collectives  22.5 us (8%)
  local copies, waits for them, and re-layouts  18.4 us (6%)
  between operations  14.9 us (5%)
  starting transfers between devices  7.77 us (3%)
    reduce_scatter x1, waiting for transfers between devices, body(): lax.psum_scatter(mine_values, 'ctx', scatter_dimension=0, tiled=True)  47.5 us
    dot_general x24, matrix products, attend(): jnp.dot(weights.astype(jnp.bfloat16), head_values, preferred_element_type...  45.9 us
    all_gather x1, waiting for transfers between devices, body(): lax.all_gather(part_keys.astype(jnp.bfloat16), 'ctx', axis=0, tiled=True)  37.4 us
    dot_general x24, matrix products, attend(): lax.dot_general(head_queries[kv_head], head_keys, (((1,), (1,)), ((), ())...  36.3 us
    all_gather x1, blocking collectives, body(): lax.all_gather(prefix_keys, 'ctx', axis=0, tiled=True)  22.5 us
    reduce_scatter x1, waiting for transfers between devices, body(): lax.psum_scatter(mine_keys, 'ctx', scatter_dimension=0, tiled=True)  21.8 us
    reduce_sum x16, other arithmetic, attend(): new_totals.append(totals[kv_head] * shrink + jnp.sum(weights, axis=1))  20.7 us
    reshape x8, local copies, waits for them, and re-layouts, body(): (accums[kv_head] / totals[kv_head][:, None]).reshape(rows_here, group_siz...  12.5 us
  transfers between devices with their start and end apart: 5, of which 3 were waited for; matrix products, arithmetic and copies ran while one was open for 24% of the time, Pallas kernels for 0%

profile of v1, /device:TPU:0, one launch (start us, length us, event | category | flops | bytes accessed | tf_op | source)
XLA Modules:
  0.0 291.9 jit_solution(1359053525430773678)
XLA Ops:
  7.3 3.9 %convert_select_fusion = (f32[512,1024]{1,0:T(8,128)}, f32[512,1024]{1,0:T(8,128)}) fusion(bf16[1,2,256,1024]{3,2,1,0:T(8,128)(2,1)} %param.15, pred[512]{0:T(512)(128)(4,1)S(1)} %broadcast_in_dim.53, bf16[1,2,256,1024]{3,2,1,0:T(8,128)(2,1)} %param.14), kind=kLoop, calls=%fused_computation.1 | loop fusion | flops 2097152 | bytes 6291968 | tf_op jit(solution)/shard_map/jit(_where)/select_n | solution.py:81
  12.7 7.5 %all-to-all-start = ((bf16[16,8,1024]{2,1,0:T(8,128)(2,1)}), bf16[16,8,1024]{2,1,0:T(8,128)(2,1)}, u32[]{:S(2)}, u32[]{:S(2)}) async-start(bf16[16,8,1024]{2,1,0:T(8,128)(2,1)} %stack.2), calls=%async_computation.2 | async-start | bytes 524288 | tf_op jit(solution)/shard_map/all_to_all | solution.py:96
  23.6 22.5 %all_gather.11 = bf16[128,1024]{1,0:T(8,128)(2,1)S(1)} all-gather(bf16[8,1024]{1,0:T(8,128)(2,1)S(1)} %copy-done.97), channel_id=1, replica_groups=mesh['groups'=2,'ctx'=16] {'ctx'}, dimensions={0}, use_global_device_ids=true | all-gather | bytes 278528 | tf_op jit(solution)/shard_map/all_gather | solution.py:94
  54.1 21.8 %reduce-scatter.3.cloned.1.call-done = f32[32,1024]{1,0:T(8,128)} async-done(((f32[512,1024]{1,0:T(8,128)}), f32[32,1024]{1,0:T(8,128)}) %reduce-scatter.3.cloned.1.call-update) | async-done | bytes 131088 | tf_op jit(solution)/shard_map/reduce_scatter | solution.py:85
  92.9 47.5 %reduce-scatter.5.cloned.1.call-done = f32[32,1024]{1,0:T(8,128)} async-done(((f32[512,1024]{1,0:T(8,128)}), f32[32,1024]{1,0:T(8,128)}) %reduce-scatter.5.cloned.1.call-update) | async-done | bytes 131088 | tf_op jit(solution)/shard_map/reduce_scatter | solution.py:86
  142.0 37.4 %all-gather.3.cloned.1.call-done = bf16[512,1024]{1,0:T(8,128)(2,1)} async-done(((bf16[32,1024]{1,0:T(8,128)(2,1)}), bf16[512,1024]{1,0:T(8,128)(2,1)}) %all-gather.3.cloned.1.call-update) | async-done | bytes 1048592 | tf_op jit(solution)/shard_map/all_gather | solution.py:89
  183.9 2.2 fusion.120
  186.0 2.9 multiply_reduce_fusion.1
  190.2 1.9 fusion.122
  210.0 1.8 fusion.124
  221.0 2.0 fusion.41
  223.0 3.3 %fusion.54 = bf16[1024,128]{1,0:T(8,128)(2,1)} fusion(f32[1024,128]{1,0:T(8,128)} %fusion.132, f32[1024,128]{1,0:T(8,128)} %fusion.41, f32[512,1024]{1,0:T(8,128)} %copy-done.6, f32[1024]{0:T(1024)S(1)} %copy-done.83, f32[1024]{0:T(1024)S(1)} %get-tuple-element.43, f32[1024]{0:T(1024)S(1)} %get-tuple-element.44, ...), kind=kOutput, calls=%fused_computation.105 | convolution fusion | flops 136445952 | bytes 3551232 | tf_op jit(solution)/shard_map/dot_general | solution.py:39
  227.4 2.1 fusion.4
  231.8 2.5 fusion.53
  236.1 2.1 fusion.6
  240.4 2.3 fusion.52
  244.5 2.1 fusion.8
  248.9 2.3 fusion.51
  252.9 2.1 fusion.10
  257.3 2.3 fusion.50
  261.4 2.1 fusion.12
  265.8 2.3 fusion.49
  274.8 2.0 fusion
  278.1 2.3 fusion.55
  (308 shorter events, 95.8 us)
Async XLA Ops:
  6.5 69.4 %reduce-scatter.3.cloned.1.call-start = ((), (), s32[]{:S(2)}) async-start(), calls=%async_computation.3 | async-start | bytes 2228224 | tf_op jit(solution)/shard_map/reduce_scatter | solution.py:85
  11.2 10.5 %copy-start.32 = (bf16[128,8192]{1,0:T(8,128)(2,1)S(1)}, bf16[128,8192]{1,0:T(8,128)(2,1)}, u32[]{:S(2)}) copy-start(bf16[128,8192]{1,0:T(8,128)(2,1)} %param.9) | copy-start | bytes 6291460
  11.3 129.2 %reduce-scatter.5.cloned.1.call-start = ((), (), s32[]{:S(2)}) async-start(), calls=%async_computation.5 | async-start | bytes 2228224 | tf_op jit(solution)/shard_map/reduce_scatter | solution.py:86
  12.7 171.1 %all-to-all-start = ((bf16[16,8,1024]{2,1,0:T(8,128)(2,1)}), bf16[16,8,1024]{2,1,0:T(8,128)(2,1)}, u32[]{:S(2)}, u32[]{:S(2)}) async-start(bf16[16,8,1024]{2,1,0:T(8,128)(2,1)} %stack.2), calls=%async_computation.2 | async-start | bytes 524288 | tf_op jit(solution)/shard_map/all_to_all | solution.py:96
  20.2 159.2 %all-gather.3.cloned.1.call-start = ((), (), s32[]{:S(2)}) async-start(), calls=%async_computation.4 | async-start | bytes 1114112 | tf_op jit(solution)/shard_map/all_gather | solution.py:89
  22.9 25.8 %copy-start.51 = (bf16[128,1024]{1,0:T(8,128)(2,1)S(1)}, bf16[128,1024]{1,0:T(8,128)(2,1)}, u32[]{:S(2)}) copy-start(bf16[128,1024]{1,0:T(8,128)(2,1)} %param.10) | copy-start | bytes 786436
  23.0 54.7 %copy-start.20 = (bf16[1024,128]{1,0:T(8,128)(2,1)}, bf16[1024,128]{1,0:T(8,128)(2,1)S(1)}, u32[]{:S(2)}) copy-start(bf16[1024,128]{1,0:T(8,128)(2,1)S(1)} %reshape.490) | copy-start | bytes 786436
  23.3 26.7 %copy-start.27 = (bf16[1024,128]{1,0:T(8,128)(2,1)}, bf16[1024,128]{1,0:T(8,128)(2,1)S(1)}, u32[]{:S(2)}) copy-start(bf16[1024,128]{1,0:T(8,128)(2,1)S(1)} %reshape.500) | copy-start | bytes 786436
  23.6 26.4 %copy-start.24 = (bf16[1024,128]{1,0:T(8,128)(2,1)}, bf16[1024,128]{1,0:T(8,128)(2,1)S(1)}, u32[]{:S(2)}) copy-start(bf16[1024,128]{1,0:T(8,128)(2,1)S(1)} %reshape.498) | copy-start | bytes 786436
  49.7 139.2 %copy-start.69 = (f32[1024]{0:T(1024)}, f32[1024]{0:T(1024)S(1)}, u32[]{:S(2)}) copy-start(f32[1024]{0:T(1024)S(1)} %get-tuple-element.95) | copy-start | bytes 12292
  50.0 130.9 %copy-start.67 = (f32[1024]{0:T(1024)}, f32[1024]{0:T(1024)S(1)}, u32[]{:S(2)}) copy-start(f32[1024]{0:T(1024)S(1)} %get-tuple-element.89) | copy-start | bytes 12292
  50.0 29.4 %copy-start.37 = (bf16[128,1024]{1,0:T(8,128)(2,1)S(1)}, bf16[128,1024]{1,0:T(8,128)(2,1)}, u32[]{:S(2)}) copy-start(bf16[128,1024]{1,0:T(8,128)(2,1)} %get-tuple-element.53) | copy-start | bytes 786436
  50.0 29.5 %copy-start.36 = (bf16[128,1024]{1,0:T(8,128)(2,1)S(1)}, bf16[128,1024]{1,0:T(8,128)(2,1)}, u32[]{:S(2)}) copy-start(bf16[128,1024]{1,0:T(8,128)(2,1)} %get-tuple-element.54) | copy-start | bytes 786436
  51.6 28.0 %copy-start.35 = (bf16[128,1024]{1,0:T(8,128)(2,1)S(1)}, bf16[128,1024]{1,0:T(8,128)(2,1)}, u32[]{:S(2)}) copy-start(bf16[128,1024]{1,0:T(8,128)(2,1)} %get-tuple-element.55) | copy-start | bytes 786436
  51.6 28.2 %copy-start.34 = (bf16[128,1024]{1,0:T(8,128)(2,1)S(1)}, bf16[128,1024]{1,0:T(8,128)(2,1)}, u32[]{:S(2)}) copy-start(bf16[128,1024]{1,0:T(8,128)(2,1)} %get-tuple-element.56) | copy-start | bytes 786436
  77.5 145.5 %all-gather.5.cloned.1.call-start = ((), (), s32[]{:S(2)}) async-start(), calls=%async_computation.6 | async-start | bytes 1114112 | tf_op jit(solution)/shard_map/all_gather | solution.py:90
  79.5 11.8 %copy-start.22 = (bf16[1024,128]{1,0:T(8,128)(2,1)}, bf16[1024,128]{1,0:T(8,128)(2,1)S(1)}, u32[]{:S(2)}) copy-start(bf16[1024,128]{1,0:T(8,128)(2,1)S(1)} %reshape.488) | copy-start | bytes 786436
  79.6 8.4 %copy-start.30 = (bf16[1024,128]{1,0:T(8,128)(2,1)}, bf16[1024,128]{1,0:T(8,128)(2,1)S(1)}, u32[]{:S(2)}) copy-start(bf16[1024,128]{1,0:T(8,128)(2,1)S(1)} %reshape.496) | copy-start | bytes 786436
  189.6 18.5 %copy-start.57 = (f32[1024]{0:T(1024)}, f32[1024]{0:T(1024)S(1)}, u32[]{:S(2)}) copy-start(f32[1024]{0:T(1024)S(1)} %get-tuple-element.64) | copy-start | bytes 12292
  194.5 13.5 %copy-start.61 = (f32[1024]{0:T(1024)}, f32[1024]{0:T(1024)S(1)}, u32[]{:S(2)}) copy-start(f32[1024]{0:T(1024)S(1)} %get-tuple-element.66) | copy-start | bytes 12292
  197.6 10.4 %copy-start.62 = (f32[1024]{0:T(1024)}, f32[1024]{0:T(1024)S(1)}, u32[]{:S(2)}) copy-start(f32[1024]{0:T(1024)S(1)} %get-tuple-element.68) | copy-start | bytes 12292
  197.6 14.3 %copy-start.52 = (f32[1024]{0:T(1024)}, f32[1024]{0:T(1024)S(1)}, u32[]{:S(2)}) copy-start(f32[1024]{0:T(1024)S(1)} %get-tuple-element.31) | copy-start | bytes 12292
  200.7 12.9 %copy-start.53 = (f32[1024]{0:T(1024)}, f32[1024]{0:T(1024)S(1)}, u32[]{:S(2)}) copy-start(f32[1024]{0:T(1024)S(1)} %get-tuple-element.36) | copy-start | bytes 12292
  203.9 11.6 %copy-start.54 = (f32[1024]{0:T(1024)}, f32[1024]{0:T(1024)S(1)}, u32[]{:S(2)}) copy-start(f32[1024]{0:T(1024)S(1)} %get-tuple-element.41) | copy-start | bytes 12292
  (81 other events, 287.2 us)
Sparse Core Ops, SparseCore 0:
  11.4 64.5 reduce-scatter.2
  79.7 60.6 reduce-scatter.4
  142.6 36.7 all-gather.2
  181.4 36.8 all-gather.4
